TPU v7x, 32 devices: a whole 2x2x4 slice. The times are simulated.
32 devices in a mesh: tile: 8 (over z, x), trace: 4 (over y, core).
Axes of the slice: x: 2, y: 2, z: 4, core: 2. Of those that a mesh axis runs over, the one named last changes fastest.
Arguments:
- traces: bfloat16 [4, 128, 32, 256], P('trace', 'tile'), may hold values from -6 to 6
- taps: bfloat16 [2, 65], replicated, may hold values from -0.75 to 0.75
- aperture: int32 [4, 8, 128], P('trace'), may hold values from 0 to 127, as said below
- counts: int32 [4, 8], P('trace'), may hold values from 32 to 128, as said below
- time_weights: bfloat16 [4, 8, 128, 128, 256], P('trace', 'tile'), may hold values from -0.375 to 0.375
- amplitudes: bfloat16 [4, 8, 128, 2, 32, 256], P('trace', 'tile'), may hold values from -0.0625 to 0.0625
Outputs:
- image: float32 [8, 128, 256], P('tile', 'trace')
Inputs may be any that keep to these rules, and one draw needn't show every extreme that they name: `aperture`: entries of one list are distinct ids of the subset's blocks; they come in runs of 16 consecutive entries whose ids share the owner index id // 16, and no owner index appears in more than one run of a list. `counts`: some list uses all 128 entries and some uses 128 // 4.
All inputs are finite; a program needn't handle non-finite values.
Results may differ from a plain program's by a relative error of at most 0.0041.
Values may be sent and summed in bfloat16 or wider, within the bound.
A program may use at most 64 MiB of HBM per device.

v0:
```python
import jax
import jax.numpy as jnp
from jax import lax
from jax.sharding import PartitionSpec as P

group_slots = 8


def filter_matrix(taps, samples):
    width = taps.shape[1]
    center = (width - 1) // 2
    offset = jnp.arange(samples)[:, None] - jnp.arange(samples)[None, :] + center
    table = (offset[:, :, None] == jnp.arange(width)[None, None, :]).astype(jnp.bfloat16)
    return jnp.einsum("ct,nmt->cnm", taps, table, preferred_element_type=jnp.float32).astype(
        jnp.bfloat16
    )


def per_device(traces, taps, aperture, counts, time_weights, amplitudes):
    tiles = lax.axis_size("tile")
    myself = lax.axis_index("tile")
    block_count = traces.shape[1]
    samples = traces.shape[3]
    slots = aperture.shape[2]
    capacity = max(2, slots // tiles)
    listing = aperture[0]
    filled = counts[0]
    owners = listing // block_count
    within = listing - owners * block_count
    order = jnp.arange(slots)
    earlier = order[None, :] < order[:, None]
    rank = jnp.sum((owners[:, :, None] == owners[:, None, :]) & earlier[None], axis=2)
    alive_slots = order[None, :] < filled[:, None]
    mine = (owners == myself) & alive_slots
    rank_onehot = (
        (rank[:, :, None] == jnp.arange(capacity)[None, None, :]) & mine[:, :, None]
    ).astype(jnp.bfloat16)
    local_onehot = (within[:, :, None] == jnp.arange(block_count)[None, None, :]).astype(
        jnp.bfloat16
    )
    select = jnp.einsum(
        "ksc,ksl->kcl", rank_onehot, local_onehot, preferred_element_type=jnp.float32
    ).astype(jnp.bfloat16)
    operator = filter_matrix(taps, samples)
    own_owner = lax.dynamic_index_in_dim(owners, myself, 0, keepdims=False)
    own_rank = lax.dynamic_index_in_dim(rank, myself, 0, keepdims=False)
    own_fill = lax.dynamic_index_in_dim(filled, myself, 0, keepdims=False)
    source_slot = own_owner * capacity + own_rank
    arrived_rows = tiles * capacity

    def pick_rows(positions):
        return (positions[:, None] == jnp.arange(arrived_rows)[None, :]).astype(jnp.bfloat16)

    filtered = jnp.einsum(
        "cnm,kbm->kcbn", operator, traces[0], preferred_element_type=jnp.float32
    ).astype(jnp.bfloat16)
    outgoing = jnp.einsum(
        "kcl,lqbn->kcqbn", select, filtered, preferred_element_type=jnp.float32
    ).astype(jnp.bfloat16)
    arrived = lax.all_to_all(outgoing, "tile", split_axis=0, concat_axis=0, tiled=True)
    arrived = arrived.reshape((arrived_rows,) + arrived.shape[2:])

    def fetch(positions):
        return jnp.einsum(
            "gq,qcbn->gcbn", pick_rows(positions), arrived, preferred_element_type=jnp.float32
        ).astype(jnp.bfloat16)

    weights = time_weights[0, 0]
    spread = amplitudes[0, 0]

    def add_group(index, total):
        start = index * group_slots
        positions = lax.dynamic_slice_in_dim(source_slot, start, group_slots, 0)
        blocks = fetch(positions)
        part_weights = lax.dynamic_slice_in_dim(weights, start, group_slots, 0)
        part_spread = lax.dynamic_slice_in_dim(spread, start, group_slots, 0)
        alive = (start + jnp.arange(group_slots) < own_fill).astype(jnp.float32)
        interp = jnp.einsum(
            "gtn,gcbn->gcbt", part_weights, blocks, preferred_element_type=jnp.float32
        )
        interp = (interp * alive[:, None, None, None]).astype(jnp.bfloat16)
        return total + jnp.einsum(
            "gcbt,gcbp->tp", interp, part_spread, preferred_element_type=jnp.float32
        )

    rounds = (own_fill + group_slots - 1) // group_slots
    partial_value = lax.fori_loop(
        0, rounds, add_group, jnp.zeros((weights.shape[1], spread.shape[-1]), jnp.float32)
    )
    image = lax.psum_scatter(partial_value, "trace", scatter_dimension=0, tiled=True)
    return image[None]


def solution(mesh):
    placed = (
        P("trace", "tile", None, None),
        P(),
        P("trace", None, None),
        P("trace", None),
        P("trace", "tile", None, None, None),
        P("trace", "tile", None, None, None, None),
    )
    return jax.shard_map(
        per_device, mesh=mesh, in_specs=placed, out_specs=P("tile", "trace", None), check_vma=False
    )
```

profile of v0, /device:TPU:0, one launch (start us, length us, event | category | flops | bytes accessed | tf_op | source)
XLA Modules:
  0.0 232.1 jit_solution(4229469800212086474)
XLA Ops:
  8.5 3.1 %fusion.19 = bf16[2,256,256,1]{2,0,1,3:T(2,128)(2,1)S(1)} fusion(s32[256,256]{1,0:T(8,128)S(1)} %subtract_add_fusion, bf16[2,65]{1,0:T(2,128)(2,1)S(1)} %copy-done), kind=kOutput, calls=%fused_computation.23 | convolution fusion | flops 21430272 | bytes 524548 | tf_op jit(solution)/shard_map/ct,nmt->cnm/dot_general | solution.py:14
  11.8 3.4 %convolution_convert_fusion.1 = bf16[8,16,2,32,256]{4,1,3,2,0:T(8,128)(2,1)} fusion(bf16[8,16,16,1,1]{2,1,4,3,0:T(8,128)(2,1)S(1)} %fusion.20, bf16[2,256,256,1]{2,0,1,3:T(2,128)(2,1)S(1)} %fusion.19, bf16[16,32,256]{2,1,0:T(8,128)(2,1)S(1)} %bitcast.81), kind=kOutput, calls=%fused_computation.19 | convolution fusion | flops 203685888 | bytes 4722688 | tf_op jit(solution)/shard_map/kcl,lqbn->kcqbn/dot_general | solution.py:57
  15.2 7.4 %all-to-all-start = ((bf16[8,16,2,32,256]{4,1,3,2,0:T(8,128)(2,1)}), bf16[8,16,2,32,256]{4,1,3,2,0:T(8,128)(2,1)}, u32[]{:S(2)}, u32[]{:S(2)}) async-start(bf16[8,16,2,32,256]{4,1,3,2,0:T(8,128)(2,1)} %convolution_convert_fusion.1), calls=%async_computation | async-start | bytes 8388608 | tf_op jit(solution)/shard_map/all_to_all | solution.py:60
  23.7 4.7 %copy.34 = bf16[1,1,128,2,32,256]{5,4,2,3,1,0:T(8,128)(2,1)} copy(bf16[1,1,128,2,32,256]{5,4,3,2,1,0:T(8,128)(2,1)} %param.13) | data formatting | bytes 8388608 | tf_op args[5]
  28.4 87.4 %all-to-all-done = bf16[8,16,2,32,256]{4,1,3,2,0:T(8,128)(2,1)} async-done(((bf16[8,16,2,32,256]{4,1,3,2,0:T(8,128)(2,1)}), bf16[8,16,2,32,256]{4,1,3,2,0:T(8,128)(2,1)}, u32[]{:S(2)}, u32[]{:S(2)}) %all-to-all-start) | async-done | bytes 4194336 | tf_op jit(solution)/shard_map/all_to_all | solution.py:60
  115.8 3.8 %copy.13 = bf16[8,16,2,32,256]{4,3,2,1,0:T(8,128)(2,1)S(1)} copy(bf16[8,16,2,32,256]{4,1,3,2,0:T(8,128)(2,1)} %all-to-all-done) | data formatting | bytes 8388608 | tf_op jit(solution)/shard_map/all_to_all | solution.py:60
  119.7 4.4 %copy.15 = bf16[128,2,32,256]{3,0,2,1:T(8,128)(2,1)} copy(bf16[128,2,32,256]{3,2,1,0:T(8,128)(2,1)S(1)} %bitcast.78) | data formatting | bytes 8388608 | tf_op jit(solution)/shard_map/while | solution.py:87
  124.1 62.3 %while.10 = (s32[]{:T(128)}, f32[128,256]{1,0:T(8,128)S(1)}, s32[]{:T(128)}, s32[128]{0:T(128)S(1)}, bf16[128,2,32,256]{3,0,2,1:T(8,128)(2,1)}, /*index=5*/bf16[...) while((s32[]{:T(128)}, f32[128,256]{1,0:T(8,128)S(1)}, ...), condition=%wide.region_2.3_spmd, body=%wide.region_1.2_spmd.sunk | while | flops 100959264 | bytes 5768527 | solution.py:87
  124.7 2.9 %convolution_convert_fusion.5 = bf16[8,2,32,256]{3,0,2,1:T(8,128)(2,1)S(1)} fusion(bf16[128,2,32,256]{3,0,2,1:T(8,128)(2,1)} %get-tuple-element.153, s32[8]{0:T(128)S(1)} %dynamic_slice.48), kind=kOutput, calls=%fused_computation.clone.1 | convolution fusion | flops 33686528 | bytes 4456480 | tf_op jit(solution)/shard_map/while/body/gq,qcbn->gcbn/dot_general | solution.py:64
  129.9 2.9 %convolution_convert_fusion.5 = bf16[8,2,32,256]{3,0,2,1:T(8,128)(2,1)S(1)} fusion(bf16[128,2,32,256]{3,0,2,1:T(8,128)(2,1)} %get-tuple-element.153, s32[8]{0:T(128)S(1)} %dynamic_slice.48), kind=kOutput, calls=%fused_computation.clone.1 | convolution fusion | flops 33686528 | bytes 4456480 | tf_op jit(solution)/shard_map/while/body/gq,qcbn->gcbn/dot_general | solution.py:64
  135.1 2.9 %convolution_convert_fusion.5 = bf16[8,2,32,256]{3,0,2,1:T(8,128)(2,1)S(1)} fusion(bf16[128,2,32,256]{3,0,2,1:T(8,128)(2,1)} %get-tuple-element.153, s32[8]{0:T(128)S(1)} %dynamic_slice.48), kind=kOutput, calls=%fused_computation.clone.1 | convolution fusion | flops 33686528 | bytes 4456480 | tf_op jit(solution)/shard_map/while/body/gq,qcbn->gcbn/dot_general | solution.py:64
  138.0 1.6 fusion.53
  140.3 2.9 %convolution_convert_fusion.5 = bf16[8,2,32,256]{3,0,2,1:T(8,128)(2,1)S(1)} fusion(bf16[128,2,32,256]{3,0,2,1:T(8,128)(2,1)} %get-tuple-element.153, s32[8]{0:T(128)S(1)} %dynamic_slice.48), kind=kOutput, calls=%fused_computation.clone.1 | convolution fusion | flops 33686528 | bytes 4456480 | tf_op jit(solution)/shard_map/while/body/gq,qcbn->gcbn/dot_general | solution.py:64
  145.5 2.9 %convolution_convert_fusion.5 = bf16[8,2,32,256]{3,0,2,1:T(8,128)(2,1)S(1)} fusion(bf16[128,2,32,256]{3,0,2,1:T(8,128)(2,1)} %get-tuple-element.153, s32[8]{0:T(128)S(1)} %dynamic_slice.48), kind=kOutput, calls=%fused_computation.clone.1 | convolution fusion | flops 33686528 | bytes 4456480 | tf_op jit(solution)/shard_map/while/body/gq,qcbn->gcbn/dot_general | solution.py:64
  150.7 2.9 %convolution_convert_fusion.5 = bf16[8,2,32,256]{3,0,2,1:T(8,128)(2,1)S(1)} fusion(bf16[128,2,32,256]{3,0,2,1:T(8,128)(2,1)} %get-tuple-element.153, s32[8]{0:T(128)S(1)} %dynamic_slice.48), kind=kOutput, calls=%fused_computation.clone.1 | convolution fusion | flops 33686528 | bytes 4456480 | tf_op jit(solution)/shard_map/while/body/gq,qcbn->gcbn/dot_general | solution.py:64
  153.6 1.6 fusion.53
  155.9 2.9 %convolution_convert_fusion.5 = bf16[8,2,32,256]{3,0,2,1:T(8,128)(2,1)S(1)} fusion(bf16[128,2,32,256]{3,0,2,1:T(8,128)(2,1)} %get-tuple-element.153, s32[8]{0:T(128)S(1)} %dynamic_slice.48), kind=kOutput, calls=%fused_computation.clone.1 | convolution fusion | flops 33686528 | bytes 4456480 | tf_op jit(solution)/shard_map/while/body/gq,qcbn->gcbn/dot_general | solution.py:64
  158.8 1.6 fusion.53
  161.1 2.9 %convolution_convert_fusion.5 = bf16[8,2,32,256]{3,0,2,1:T(8,128)(2,1)S(1)} fusion(bf16[128,2,32,256]{3,0,2,1:T(8,128)(2,1)} %get-tuple-element.153, s32[8]{0:T(128)S(1)} %dynamic_slice.48), kind=kOutput, calls=%fused_computation.clone.1 | convolution fusion | flops 33686528 | bytes 4456480 | tf_op jit(solution)/shard_map/while/body/gq,qcbn->gcbn/dot_general | solution.py:64
  166.3 2.9 %convolution_convert_fusion.5 = bf16[8,2,32,256]{3,0,2,1:T(8,128)(2,1)S(1)} fusion(bf16[128,2,32,256]{3,0,2,1:T(8,128)(2,1)} %get-tuple-element.153, s32[8]{0:T(128)S(1)} %dynamic_slice.48), kind=kOutput, calls=%fused_computation.clone.1 | convolution fusion | flops 33686528 | bytes 4456480 | tf_op jit(solution)/shard_map/while/body/gq,qcbn->gcbn/dot_general | solution.py:64
  171.5 2.9 %convolution_convert_fusion.5 = bf16[8,2,32,256]{3,0,2,1:T(8,128)(2,1)S(1)} fusion(bf16[128,2,32,256]{3,0,2,1:T(8,128)(2,1)} %get-tuple-element.153, s32[8]{0:T(128)S(1)} %dynamic_slice.48), kind=kOutput, calls=%fused_computation.clone.1 | convolution fusion | flops 33686528 | bytes 4456480 | tf_op jit(solution)/shard_map/while/body/gq,qcbn->gcbn/dot_general | solution.py:64
  176.6 2.9 %convolution_convert_fusion.5 = bf16[8,2,32,256]{3,0,2,1:T(8,128)(2,1)S(1)} fusion(bf16[128,2,32,256]{3,0,2,1:T(8,128)(2,1)} %get-tuple-element.153, s32[8]{0:T(128)S(1)} %dynamic_slice.48), kind=kOutput, calls=%fused_computation.clone.1 | convolution fusion | flops 33686528 | bytes 4456480 | tf_op jit(solution)/shard_map/while/body/gq,qcbn->gcbn/dot_general | solution.py:64
  181.8 2.9 %convolution_convert_fusion.5 = bf16[8,2,32,256]{3,0,2,1:T(8,128)(2,1)S(1)} fusion(bf16[128,2,32,256]{3,0,2,1:T(8,128)(2,1)} %get-tuple-element.153, s32[8]{0:T(128)S(1)} %dynamic_slice.48), kind=kOutput, calls=%fused_computation.clone.1 | convolution fusion | flops 33686528 | bytes 4456480 | tf_op jit(solution)/shard_map/while/body/gq,qcbn->gcbn/dot_general | solution.py:64
  187.1 38.2 %reduce-scatter.2.cloned.1.call-done = f32[32,256]{1,0:T(8,128)} async-done(((f32[128,256]{1,0:T(8,128)}), f32[32,256]{1,0:T(8,128)}) %reduce-scatter.2.cloned.1.call-update) | async-done | bytes 32784 | tf_op jit(solution)/shard_map/reduce_scatter | solution.py:90
  (52 shorter events, 25.7 us)
Async XLA Ops:
  6.5 1.9 copy-start
  6.5 5.2 %copy-start.2 = (bf16[1,16,32,256]{3,2,1,0:T(8,128)(2,1)S(1)}, bf16[1,16,32,256]{3,2,1,0:T(8,128)(2,1)}, u32[]{:S(2)}) copy-start(bf16[1,16,32,256]{3,2,1,0:T(8,128)(2,1)} %param.8) | copy-start | bytes 786436
  15.2 7.4 %copy-start.3 = (s32[1,8]{1,0:T(1,128)S(1)}, s32[1,8]{1,0:T(1,128)}, u32[]{:S(2)}) copy-start(s32[1,8]{1,0:T(1,128)} %param.11) | copy-start | bytes 100
  15.2 100.7 %all-to-all-start = ((bf16[8,16,2,32,256]{4,1,3,2,0:T(8,128)(2,1)}), bf16[8,16,2,32,256]{4,1,3,2,0:T(8,128)(2,1)}, u32[]{:S(2)}, u32[]{:S(2)}) async-start(bf16[8,16,2,32,256]{4,1,3,2,0:T(8,128)(2,1)} %convolution_convert_fusion.1), calls=%async_computation | async-start | bytes 8388608 | tf_op jit(solution)/shard_map/all_to_all | solution.py:60
  22.5 202.7 %reduce-scatter.2.cloned.1.call-start = ((), (), s32[]{:S(2)}) async-start(), calls=%async_computation.2 | async-start | bytes 163840 | tf_op jit(solution)/shard_map/reduce_scatter | solution.py:90
  186.4 0.6 copy-start.1
Sparse Core Ops, SparseCore 0:
  187.2 38.0 reduce-scatter.1
where the time goes:
time: 233 us; the launch traced here: 232 us
  waiting for transfers between devices  126 us (54%)
  matrix products  61 us (26%)
  local copies, waits for them, and re-layouts  15.1 us (6%)
  between operations  14 us (6%)
  other arithmetic  8.51 us (4%)
  starting transfers between devices  7.42 us (3%)
    all_to_all x1, waiting for transfers between devices, per_device(): lax.all_to_all(outgoing, 'tile', split_axis=0, concat_axis=0, tiled=True)  87.4 us
    reduce_scatter x1, waiting for transfers between devices, per_device(): lax.psum_scatter(partial_value, 'trace', scatter_dimension=0, tiled=True)  38.2 us
    dot_general x12, matrix products, fetch(): jnp.einsum('gq,qcbn->gcbn', pick_rows(positions), arrived, preferred_elem...  34.5 us
    dot_general x12, matrix products, add_group(): jnp.einsum('gcbt,gcbp->tp', interp, part_spread, preferred_element_type=j...  19.8 us
    all_to_all x1, starting transfers between devices, per_device(): lax.all_to_all(outgoing, 'tile', split_axis=0, concat_axis=0, tiled=True)  7.39 us
    convert_element_type x12, other arithmetic, add_group(): alive = (start + jnp.arange(group_slots) < own_fill).astype(jnp.float32)  6.59 us
    unnamed x9, local copies, waits for them, and re-layouts  5.31 us
  transfers between devices with their start and end apart: 2, of which 2 were waited for; matrix products, arithmetic and copies ran while one was open for 2% of the time, Pallas kernels for 0%

commit v1 on v0

--- a/solution.py
+++ b/solution.py
@@ -1,9 +1,334 @@
+import functools
+
 import jax
 import jax.numpy as jnp
 from jax import lax
+from jax.experimental import pallas as pl
+from jax.experimental.pallas import tpu as pltpu
 from jax.sharding import PartitionSpec as P
 
 group_slots = 8
+lane_group = 4
+halves = 2
+MESH = pl.DeviceIdType.MESH
+
+
+def migrate_kernel(
+    rows_z,
+    subsets,
+    half_taps,
+    inv_ref,
+    alive_ref,
+    band_ref,
+    traces_ref,
+    weights_ref,
+    spread_ref,
+    out_ref,
+    gathered,
+    weights,
+    spread,
+    operator,
+    filtered,
+    total,
+    parts,
+    recv_sem,
+    send_z_sem,
+    send_x_sem,
+    load_sem,
+    part_send_sem,
+    part_recv_sem,
+):
+    tile = lax.axis_index("tile")
+    subset = lax.axis_index("trace")
+    z = tile // 2
+    x = tile % 2
+    other = 1 - x
+    samples = operator.shape[1]
+    chunk_rows = gathered.shape[2]
+    block_rows = spread.shape[2]
+    chunk_blocks = chunk_rows // block_rows
+    block_count = chunk_blocks * halves
+    group_lanes = lane_group * block_rows
+
+    load_own = pltpu.make_async_copy(traces_ref, gathered.at[tile], load_sem.at[0])
+    load_weights = pltpu.make_async_copy(weights_ref, weights, load_sem.at[1])
+    load_spread = pltpu.make_async_copy(spread_ref, spread, load_sem.at[2])
+
+    barrier = pltpu.get_barrier_semaphore()
+
+    @pl.when(z > 0)
+    def _():
+        pl.semaphore_signal(barrier, inc=1, device_id=(tile - 2, subset), device_id_type=MESH)
+
+    @pl.when(z < rows_z - 1)
+    def _():
+        pl.semaphore_signal(barrier, inc=1, device_id=(tile + 2, subset), device_id_type=MESH)
+
+    pl.semaphore_signal(barrier, inc=1, device_id=(z * 2 + other, subset), device_id_type=MESH)
+    for step in range(1, subsets):
+        pl.semaphore_signal(
+            barrier, inc=1, device_id=(tile, (subset + step) % subsets), device_id_type=MESH
+        )
+    load_own.start()
+    load_weights.start()
+    load_spread.start()
+    inner = jnp.where((z > 0) & (z < rows_z - 1), 1, 0)
+    pl.semaphore_wait(barrier, subsets + 1 + inner)
+
+    def source(origin_z, half, own):
+        if own:
+            return traces_ref.at[half]
+        return gathered.at[origin_z * 2 + x, half]
+
+    def send_z(origin_z, half, up, own=False):
+        return pltpu.make_async_remote_copy(
+            src_ref=source(origin_z, half, own),
+            dst_ref=gathered.at[origin_z * 2 + x, half],
+            send_sem=send_z_sem.at[up, origin_z, half],
+            recv_sem=recv_sem.at[origin_z * 2 + x, half],
+            device_id=(tile + 4 * up - 2, subset),
+            device_id_type=MESH,
+        )
+
+    def send_x(origin_z, half, own=False):
+        return pltpu.make_async_remote_copy(
+            src_ref=source(origin_z, half, own),
+            dst_ref=gathered.at[origin_z * 2 + x, half],
+            send_sem=send_x_sem.at[origin_z, half],
+            recv_sem=recv_sem.at[origin_z * 2 + x, half],
+            device_id=(z * 2 + other, subset),
+            device_id_type=MESH,
+        )
+
+    def wait_arrival(origin, half):
+        pltpu.make_async_remote_copy(
+            src_ref=gathered.at[origin, half],
+            dst_ref=gathered.at[origin, half],
+            send_sem=send_x_sem.at[0, 0],
+            recv_sem=recv_sem.at[origin, half],
+            device_id=(z * 2 + other, subset),
+            device_id_type=MESH,
+        ).wait_recv()
+
+    for half in range(halves):
+
+        @pl.when(z < rows_z - 1)
+        def _():
+            send_z(z, half, 1, True).start()
+
+        @pl.when(z > 0)
+        def _():
+            send_z(z, half, 0, True).start()
+
+        send_x(z, half, True).start()
+
+    row = lax.broadcasted_iota(jnp.int32, (samples, samples), 0)
+    gap = lax.broadcasted_iota(jnp.int32, (samples, samples), 1) - row
+    inside = (gap <= half_taps) & (gap >= -half_taps)
+    for channel in range(2):
+        band = jnp.broadcast_to(band_ref[channel : channel + 1, :], (samples, samples))
+        shift = 1
+        while shift < samples:
+            band = jnp.where((row // shift) % 2 == 1, pltpu.roll(band, shift, 1), band)
+            shift *= 2
+        operator[channel * samples : (channel + 1) * samples, :] = jnp.where(
+            inside, band, 0.0
+        ).astype(operator.dtype)
+    total[...] = jnp.zeros_like(total)
+
+    lanes = lax.broadcasted_iota(jnp.int32, (1, 2 * group_lanes), 1)
+    member = (lanes // block_rows) % lane_group
+
+    def compute(origin, half):
+        filtered[...] = lax.dot_general(
+            operator[...],
+            gathered[origin, half],
+            (((1,), (1,)), ((), ())),
+            preferred_element_type=jnp.float32,
+        ).astype(filtered.dtype)
+        taus = weights.shape[1]
+        for group in range(chunk_blocks // lane_group):
+            first = group * group_lanes
+            blocks = jnp.concatenate(
+                [
+                    filtered[0:samples, first : first + group_lanes],
+                    filtered[samples : 2 * samples, first : first + group_lanes],
+                ],
+                axis=1,
+            )
+            base = origin * block_count + half * chunk_blocks + group * lane_group
+            slots = [inv_ref[base + index] for index in range(lane_group)]
+            stacked = jnp.concatenate([weights[slot] for slot in slots], axis=0)
+            product = jnp.dot(stacked, blocks, preferred_element_type=jnp.float32)
+            interp = product[0:taus]
+            alive = jnp.full((1, 2 * group_lanes), alive_ref[base], jnp.float32)
+            for index in range(1, lane_group):
+                here = member == index
+                interp = jnp.where(here, product[index * taus : (index + 1) * taus], interp)
+                alive = jnp.where(here, alive_ref[base + index], alive)
+            interp = (interp * alive).astype(jnp.bfloat16)
+            columns = jnp.concatenate(
+                [spread[slot, channel] for channel in range(2) for slot in slots], axis=0
+            )
+            total[...] += jnp.dot(interp, columns, preferred_element_type=jnp.float32)
+
+    load_own.wait()
+    load_weights.wait()
+    load_spread.wait()
+
+    def own_chunk(half, carry):
+        compute(tile, half)
+        return carry
+
+    lax.fori_loop(0, halves, own_chunk, 0)
+
+    for distance in range(1, rows_z + 1):
+        for half in range(halves):
+            for up in (1, 0):
+                origin_z = z - distance if up else z + distance
+
+                @pl.when((origin_z >= 0) & (origin_z < rows_z))
+                def _():
+                    wait_arrival(origin_z * 2 + x, half)
+
+                    @pl.when((z > 0) & (z < rows_z - 1))
+                    def _():
+                        send_z(origin_z, half, up).start()
+
+                    send_x(origin_z, half).start()
+
+        def column_chunk(event, carry):
+            half = event // 2
+            up = event % 2
+            near = z - distance * (2 * up - 1)
+            far = z - (distance - 1) * (2 * up - 1)
+
+            @pl.when((near >= 0) & (near < rows_z))
+            def _():
+                compute(near * 2 + x, half)
+
+            if distance > 1:
+                wanted = (far >= 0) & (far < rows_z)
+            else:
+                wanted = up == 1
+
+            @pl.when(wanted)
+            def _():
+                wait_arrival(far * 2 + other, half)
+                compute(far * 2 + other, half)
+
+            return carry
+
+        lax.fori_loop(0, 2 * halves, column_chunk, 0)
+
+    share = out_ref.shape[0]
+    sends = []
+    for step in range(1, subsets):
+        peer = (subset + step) % subsets
+        copy = pltpu.make_async_remote_copy(
+            src_ref=total.at[pl.ds(pl.multiple_of(peer * share, share), share)],
+            dst_ref=parts.at[step - 1],
+            send_sem=part_send_sem.at[step - 1],
+            recv_sem=part_recv_sem.at[step - 1],
+            device_id=(tile, peer),
+            device_id_type=MESH,
+        )
+        copy.start()
+        sends.append(copy)
+    result = total[pl.ds(pl.multiple_of(subset * share, share), share), :]
+    for step in range(1, subsets):
+        sends[step - 1].wait_recv()
+        result = result + parts[step - 1]
+    out_ref[...] = result
+    for copy in sends:
+        copy.wait_send()
+
+    for half in range(halves):
+
+        @pl.when(z < rows_z - 1)
+        def _():
+            send_z(z, half, 1, True).wait_send()
+
+        @pl.when(z > 0)
+        def _():
+            send_z(z, half, 0, True).wait_send()
+
+        send_x(z, half, True).wait_send()
+        for distance in range(1, rows_z):
+            for up in (1, 0):
+                origin_z = z - distance if up else z + distance
+
+                @pl.when((origin_z >= 0) & (origin_z < rows_z))
+                def _():
+                    @pl.when((z > 0) & (z < rows_z - 1))
+                    def _():
+                        send_z(origin_z, half, up).wait_send()
+
+                    send_x(origin_z, half).wait_send()
+
+
+def gather_per_device(traces, taps, aperture, counts, time_weights, amplitudes):
+    tiles = lax.axis_size("tile")
+    subsets = lax.axis_size("trace")
+    myself = lax.axis_index("tile")
+    _, block_count, block_rows, samples = traces.shape
+    slots, taus = time_weights.shape[2:4]
+    columns = amplitudes.shape[-1]
+    half_taps = (taps.shape[1] - 1) // 2
+    listing = lax.dynamic_index_in_dim(aperture[0], myself, 0, keepdims=False)
+    fill = lax.dynamic_index_in_dim(counts[0], myself, 0, keepdims=False)
+    order = jnp.arange(slots, dtype=jnp.int32)
+    blocks = jnp.arange(tiles * block_count, dtype=jnp.int32)
+    match = (listing[None, :] == blocks[:, None]) & (order < fill)[None, :]
+    inv = jnp.sum(jnp.where(match, order[None, :], 0), axis=1, dtype=jnp.int32)
+    alive = jnp.sum(match.astype(jnp.float32), axis=1)
+    flipped = taps[:, ::-1].astype(jnp.float32)
+    band = jnp.concatenate(
+        [
+            flipped[:, half_taps:],
+            jnp.zeros((2, samples - taps.shape[1]), jnp.float32),
+            flipped[:, :half_taps],
+        ],
+        axis=1,
+    )
+    chunk_rows = block_count * block_rows // halves
+    share = taus // subsets
+    rows_z = tiles // 2
+    smem = pl.BlockSpec(memory_space=pltpu.SMEM)
+    vmem = pl.BlockSpec(memory_space=pltpu.VMEM)
+    hbm = pl.BlockSpec(memory_space=pl.ANY)
+    image = pl.pallas_call(
+        functools.partial(migrate_kernel, rows_z, subsets, half_taps),
+        out_shape=jax.ShapeDtypeStruct((share, columns), jnp.float32),
+        in_specs=[smem, smem, vmem, hbm, hbm, hbm],
+        out_specs=vmem,
+        scratch_shapes=[
+            pltpu.VMEM((tiles, halves, chunk_rows, samples), jnp.bfloat16),
+            pltpu.VMEM((slots, taus, samples), jnp.bfloat16),
+            pltpu.VMEM((slots, 2, block_rows, columns), jnp.bfloat16),
+            pltpu.VMEM((2 * samples, samples), jnp.bfloat16),
+            pltpu.VMEM((2 * samples, chunk_rows), jnp.bfloat16),
+            pltpu.VMEM((taus, columns), jnp.float32),
+            pltpu.VMEM((subsets - 1, share, columns), jnp.float32),
+            pltpu.SemaphoreType.DMA((tiles, halves)),
+            pltpu.SemaphoreType.DMA((2, rows_z, halves)),
+            pltpu.SemaphoreType.DMA((rows_z, halves)),
+            pltpu.SemaphoreType.DMA((3,)),
+            pltpu.SemaphoreType.DMA((subsets - 1,)),
+            pltpu.SemaphoreType.DMA((subsets - 1,)),
+        ],
+        compiler_params=pltpu.CompilerParams(
+            collective_id=0, has_side_effects=True, vmem_limit_bytes=48 * 1024 * 1024
+        ),
+    )(
+        inv,
+        alive,
+        band,
+        traces.reshape(halves, chunk_rows, samples),
+        time_weights[0, 0],
+        amplitudes[0, 0],
+    )
+    return image[None]
 
 
 def filter_matrix(taps, samples):
@@ -16,7 +341,7 @@
     )
 
 
-def per_device(traces, taps, aperture, counts, time_weights, amplitudes):
+def exchange_per_device(traces, taps, aperture, counts, time_weights, amplitudes):
     tiles = lax.axis_size("tile")
     myself = lax.axis_index("tile")
     block_count = traces.shape[1]
@@ -91,6 +416,13 @@
     return image[None]
 
 
+def per_device(traces, taps, aperture, counts, time_weights, amplitudes):
+    tiles = lax.axis_size("tile")
+    every_block = traces.shape[1] * tiles
+    form = gather_per_device if every_block == aperture.shape[2] else exchange_per_device
+    return form(traces, taps, aperture, counts, time_weights, amplitudes)
+
+
 def solution(mesh):
     placed = (
         P("trace", "tile", None, None),

time: 233 us -> 40.6 us (0.17)
  waiting for transfers between devices: 126 us -> 0 us
  matrix products: 61 us -> 0 us
  Pallas kernels: 0 us -> 33.4 us
  between operations: 14 us -> 0.05 us
  local copies, waits for them, and re-layouts: 15.1 us -> 5.92 us
  other arithmetic: 8.51 us -> 0.94 us
  starting transfers between devices: 7.42 us -> 0 us
    all_to_all x1 -> x0, waiting for transfers between devices: 87.4 us -> none  [per_device(): lax.all_to_all(outgoing, 'tile', split_axis=0, concat_axis=0, tiled=True)]
    dot_general x27 -> x0, matrix products: 61 us -> none  [the longest x12 34.5 us: fetch(): jnp.einsum('gq,qcbn->gcbn', pick_rows(positions), arrived, preferred_elem...]
    reduce_scatter x1 -> x0, waiting for transfers between devices: 38.2 us -> none  [per_device(): lax.psum_scatter(partial_value, 'trace', scatter_dimension=0, tiled=True)]
    pallas_call x0 -> x1, Pallas kernels: none -> 33.4 us  [gather_per_device(): pl.pallas_call(functools.partial(migrate_kernel, rows_z, subsets, half_ta...]
    all_to_all x1 -> x0, starting transfers between devices: 7.39 us -> none  [per_device(): lax.all_to_all(outgoing, 'tile', split_axis=0, concat_axis=0, tiled=True)]
    convert_element_type x12 -> x0, other arithmetic: 6.59 us -> none  [add_group(): alive = (start + jnp.arange(group_slots) < own_fill).astype(jnp.float32)]
    while x1 -> x0, local copies, waits for them, and re-layouts: 4.41 us -> none  [per_device(): lax.fori_loop(0, rounds, add_group, jnp.zeros((weights.shape[1], spread.s...]
    all_to_all x1 -> x0, local copies, waits for them, and re-layouts: 3.82 us -> none  [per_device(): lax.all_to_all(outgoing, 'tile', split_axis=0, concat_axis=0, tiled=True)]
  transfers between devices with their start and end apart: 2 -> 0, of which waited for: 2 -> 0; matrix products, arithmetic and copies ran while one was open for 2% -> 0% of each run, Pallas kernels for 0% -> 0%
where the time goes in v1:
time: 40.6 us; the launch traced here: 40.3 us
  Pallas kernels  33.4 us (82%)
  local copies, waits for them, and re-layouts  5.92 us (15%)
  other arithmetic  0.94 us (2%)
    pallas_call x1, Pallas kernels, gather_per_device(): pl.pallas_call(functools.partial(migrate_kernel, rows_z, subsets, half_ta...  33.4 us
    unnamed x7, local copies, waits for them, and re-layouts  3.76 us
    dynamic_slice x1, local copies, waits for them, and re-layouts, gather_per_device(): fill = lax.dynamic_index_in_dim(counts[0], myself, 0, keepdims=False)  1.25 us

profile of v1, /device:TPU:0, one launch (start us, length us, event | category | flops | bytes accessed | tf_op | source)
XLA Modules:
  0.0 40.3 jit_solution(5916467765588273201)
XLA Ops:
  0.0 0.0 copy-start
  0.0 1.2 %constant_dynamic-slice_fusion = s32[1,1]{1,0:T(1,128)} fusion(s32[1,8]{1,0:T(1,128)} %param.9, s32[]{:T(128)S(6)} %select_n.10), kind=kLoop, calls=%fused_computation.7 | loop fusion | bytes 12 | tf_op jit(solution)/shard_map/jit(dynamic_index_in_dim)/dynamic_slice | solution.py:279
  1.3 0.6 %iota_compare_fusion.1 = pred[128]{0:T(512)(128)(4,1)S(1)} fusion(s32[]{:T(128)} %bitcast.1), kind=kLoop, calls=%fused_computation.5 | loop fusion | flops 128 | bytes 132 | tf_op jit(solution)/shard_map/lt | solution.py:282
  1.9 0.0 copy-done
  1.9 0.7 %rev.3 = bf16[2,65]{1,0:T(2,128)(2,1)S(1)} reverse(bf16[2,65]{1,0:T(2,128)(2,1)} %param.7), dimensions={1} | reverse | bytes 520 | tf_op jit(solution)/shard_map/rev | solution.py:285
  2.7 0.1 convert_reduce_fusion.alive_ref
  2.8 0.1 select_reduce_fusion.inv_ref
  2.9 0.1 slice.6
  3.0 0.1 pad.1.clone
  3.1 0.1 pad_maximum_fusion.band_ref
  3.2 0.0 copy-start.1
  3.2 2.2 %copy-done.1 = bf16[1,1,128,2,32,256]{5,4,3,2,1,0:T(8,128)(2,1)S(1)} copy-done((bf16[1,1,128,2,32,256]{5,4,3,2,1,0:T(8,128)(2,1)S(1)}, bf16[1,1,128,2,32,256]{5,4,3,2,1,0:T(8,128)(2,1)}, u32[]{:S(2)}) %copy-start.1) | copy-done | bytes 4194328
  5.3 0.0 copy-start.2
  5.3 0.9 %copy-done.2 = bf16[1,16,32,256]{3,2,1,0:T(8,128)(2,1)S(1)} copy-done((bf16[1,16,32,256]{3,2,1,0:T(8,128)(2,1)S(1)}, bf16[1,16,32,256]{3,2,1,0:T(8,128)(2,1)}, u32[]{:S(2)}) %copy-start.2) | copy-done | bytes 262168
  6.3 33.4 %shard_map.64 = f32[32,256]{1,0:T(8,128)S(1)} custom-call(s32[128]{0:T(128)S(1)} %select_reduce_fusion.inv_ref, f32[128]{0:T(128)S(1)} %convert_reduce_fusion.alive_ref, f32[2,256]{1,0:T(2,128)S(1)} %pad_maximum_fusion.band_ref, bf16[2,256,256]{2,1,0:T(8,128)(2,1)S(1)} %bitcast.8, bf16[128,128,256]{2,1,0:T(8,128)(2,1)} %bitcast.10, ...), custom_call_target="tpu_custom_call" | custom-call | tf_op jit(solution)/shard_map/pallas_call | solution.py:300
  39.7 0.6 %copy.8 = f32[1,32,256]{2,1,0:T(8,128)} copy(f32[1,32,256]{2,1,0:T(8,128)S(1)} %bitcast.9) | data formatting | bytes 65536
  (3 shorter events, 0.0 us)
Async XLA Ops:
  0.0 1.9 %copy-start = (s32[1,8,128]{2,1,0:T(8,128)S(1)}, s32[1,8,128]{2,1,0:T(8,128)}, u32[]{:S(2)}) copy-start(s32[1,8,128]{2,1,0:T(8,128)} %param.8) | copy-start | bytes 12292
  3.2 2.2 %copy-start.1 = (bf16[1,1,128,2,32,256]{5,4,3,2,1,0:T(8,128)(2,1)S(1)}, bf16[1,1,128,2,32,256]{5,4,3,2,1,0:T(8,128)(2,1)}, u32[]{:S(2)}) copy-start(bf16[1,1,128,2,32,256]{5,4,3,2,1,0:T(8,128)(2,1)} %param.11) | copy-start | bytes 12582916
  5.3 0.9 %copy-start.2 = (bf16[1,16,32,256]{3,2,1,0:T(8,128)(2,1)S(1)}, bf16[1,16,32,256]{3,2,1,0:T(8,128)(2,1)}, u32[]{:S(2)}) copy-start(bf16[1,16,32,256]{3,2,1,0:T(8,128)(2,1)} %param.6) | copy-start | bytes 786436

commit v2 on v1

--- a/solution.py
+++ b/solution.py
@@ -10,16 +10,16 @@
 group_slots = 8
 lane_group = 4
 halves = 2
+relay_from = 1
 MESH = pl.DeviceIdType.MESH
 
 
 def migrate_kernel(
     rows_z,
     subsets,
-    half_taps,
-    inv_ref,
-    alive_ref,
-    band_ref,
+    counts_hbm,
+    aperture_hbm,
+    taps_hbm,
     traces_ref,
     weights_ref,
     spread_ref,
@@ -31,9 +31,16 @@
     filtered,
     total,
     parts,
+    counts_ref,
+    aperture_ref,
+    taps_ref,
+    band,
+    lookup,
+    slot_of,
     recv_sem,
     send_z_sem,
     send_x_sem,
+    relay_sem,
     load_sem,
     part_send_sem,
     part_recv_sem,
@@ -50,6 +57,12 @@
     block_count = chunk_blocks * halves
     group_lanes = lane_group * block_rows
 
+    load_small = [
+        pltpu.make_async_copy(src, dst, load_sem.at[4 + at])
+        for at, (src, dst) in enumerate(
+            ((counts_hbm, counts_ref), (aperture_hbm, aperture_ref), (taps_hbm, taps_ref))
+        )
+    ]
     load_own = pltpu.make_async_copy(traces_ref, gathered.at[tile], load_sem.at[0])
     load_weights = pltpu.make_async_copy(weights_ref, weights, load_sem.at[1])
     load_spread = pltpu.make_async_copy(spread_ref, spread, load_sem.at[2])
@@ -69,9 +82,9 @@
         pl.semaphore_signal(
             barrier, inc=1, device_id=(tile, (subset + step) % subsets), device_id_type=MESH
         )
+    for load in load_small:
+        load.start()
     load_own.start()
-    load_weights.start()
-    load_spread.start()
     inner = jnp.where((z > 0) & (z < rows_z - 1), 1, 0)
     pl.semaphore_wait(barrier, subsets + 1 + inner)
 
@@ -97,6 +110,18 @@
             send_sem=send_x_sem.at[origin_z, half],
             recv_sem=recv_sem.at[origin_z * 2 + x, half],
             device_id=(z * 2 + other, subset),
+            device_id_type=MESH,
+        )
+
+    pair_z = z + 1 - 2 * (z % 2)
+
+    def relay(half):
+        return pltpu.make_async_remote_copy(
+            src_ref=gathered.at[z * 2 + other, half],
+            dst_ref=gathered.at[z * 2 + other, half],
+            send_sem=relay_sem.at[half],
+            recv_sem=recv_sem.at[z * 2 + other, half],
+            device_id=(pair_z * 2 + x, subset),
             device_id_type=MESH,
         )
 
@@ -122,17 +147,37 @@
 
         send_x(z, half, True).start()
 
+    load_weights.start()
+    load_spread.start()
+    for load in load_small:
+        load.wait()
+    slots = weights.shape[0]
+    listing = aperture_ref[0, pl.ds(tile, 1), :]
+    slot = lax.broadcasted_iota(jnp.int32, (slots, slots), 0)
+    block = lax.broadcasted_iota(jnp.int32, (slots, slots), 1)
+    named = jnp.broadcast_to(listing, (slots, slots)).T
+    match = (named == block) & (slot < counts_ref[0, tile])
+    lookup[...] = jnp.broadcast_to(
+        jnp.sum(jnp.where(match, slot + 1, 0), axis=0, keepdims=True) - 1, lookup.shape
+    )
+    publish = pltpu.make_async_copy(lookup, slot_of, load_sem.at[3])
+    publish.start()
+
+    half_taps = (taps_ref.shape[1] - 1) // 2
+    band[...] = jnp.zeros_like(band)
+    band[0:2, 0 : taps_ref.shape[1]] = taps_ref[...].astype(jnp.float32)
     row = lax.broadcasted_iota(jnp.int32, (samples, samples), 0)
     gap = lax.broadcasted_iota(jnp.int32, (samples, samples), 1) - row
     inside = (gap <= half_taps) & (gap >= -half_taps)
     for channel in range(2):
-        band = jnp.broadcast_to(band_ref[channel : channel + 1, :], (samples, samples))
+        centred = pltpu.roll(band[...], samples - half_taps, 1)[channel : channel + 1, :]
+        shifted = jnp.broadcast_to(centred, (samples, samples))
         shift = 1
         while shift < samples:
-            band = jnp.where((row // shift) % 2 == 1, pltpu.roll(band, shift, 1), band)
+            shifted = jnp.where((row // shift) % 2 == 1, pltpu.roll(shifted, shift, 1), shifted)
             shift *= 2
-        operator[channel * samples : (channel + 1) * samples, :] = jnp.where(
-            inside, band, 0.0
+        operator[channel * samples : (channel + 1) * samples, :] = (
+            jnp.where(inside, shifted, 0.0).T
         ).astype(operator.dtype)
     total[...] = jnp.zeros_like(total)
 
@@ -157,24 +202,27 @@
                 axis=1,
             )
             base = origin * block_count + half * chunk_blocks + group * lane_group
-            slots = [inv_ref[base + index] for index in range(lane_group)]
-            stacked = jnp.concatenate([weights[slot] for slot in slots], axis=0)
+            found = [slot_of[0, base + index] for index in range(lane_group)]
+            picks = [jnp.maximum(value, 0) for value in found]
+            gains = [jnp.where(value >= 0, 1.0, 0.0) for value in found]
+            stacked = jnp.concatenate([weights[pick] for pick in picks], axis=0)
             product = jnp.dot(stacked, blocks, preferred_element_type=jnp.float32)
             interp = product[0:taus]
-            alive = jnp.full((1, 2 * group_lanes), alive_ref[base], jnp.float32)
+            alive = jnp.full((1, 2 * group_lanes), gains[0], jnp.float32)
             for index in range(1, lane_group):
                 here = member == index
                 interp = jnp.where(here, product[index * taus : (index + 1) * taus], interp)
-                alive = jnp.where(here, alive_ref[base + index], alive)
+                alive = jnp.where(here, gains[index], alive)
             interp = (interp * alive).astype(jnp.bfloat16)
             columns = jnp.concatenate(
-                [spread[slot, channel] for channel in range(2) for slot in slots], axis=0
+                [spread[pick, channel] for channel in range(2) for pick in picks], axis=0
             )
             total[...] += jnp.dot(interp, columns, preferred_element_type=jnp.float32)
 
     load_own.wait()
     load_weights.wait()
     load_spread.wait()
+    publish.wait()
 
     def own_chunk(half, carry):
         compute(tile, half)
@@ -195,7 +243,17 @@
                     def _():
                         send_z(origin_z, half, up).start()
 
-                    send_x(origin_z, half).start()
+                    if half < relay_from:
+                        send_x(origin_z, half).start()
+                    else:
+
+                        @pl.when(origin_z != pair_z)
+                        def _():
+                            send_x(origin_z, half).start()
+
+        if distance == 2:
+            for half in range(relay_from, halves):
+                relay(half).start()
 
         def column_chunk(event, carry):
             half = event // 2
@@ -264,43 +322,33 @@
                     def _():
                         send_z(origin_z, half, up).wait_send()
 
-                    send_x(origin_z, half).wait_send()
+                    if half < relay_from:
+                        send_x(origin_z, half).wait_send()
+                    else:
+
+                        @pl.when(origin_z != pair_z)
+                        def _():
+                            send_x(origin_z, half).wait_send()
+
+    for half in range(relay_from, halves):
+        relay(half).wait_send()
 
 
 def gather_per_device(traces, taps, aperture, counts, time_weights, amplitudes):
     tiles = lax.axis_size("tile")
     subsets = lax.axis_size("trace")
-    myself = lax.axis_index("tile")
     _, block_count, block_rows, samples = traces.shape
     slots, taus = time_weights.shape[2:4]
     columns = amplitudes.shape[-1]
-    half_taps = (taps.shape[1] - 1) // 2
-    listing = lax.dynamic_index_in_dim(aperture[0], myself, 0, keepdims=False)
-    fill = lax.dynamic_index_in_dim(counts[0], myself, 0, keepdims=False)
-    order = jnp.arange(slots, dtype=jnp.int32)
-    blocks = jnp.arange(tiles * block_count, dtype=jnp.int32)
-    match = (listing[None, :] == blocks[:, None]) & (order < fill)[None, :]
-    inv = jnp.sum(jnp.where(match, order[None, :], 0), axis=1, dtype=jnp.int32)
-    alive = jnp.sum(match.astype(jnp.float32), axis=1)
-    flipped = taps[:, ::-1].astype(jnp.float32)
-    band = jnp.concatenate(
-        [
-            flipped[:, half_taps:],
-            jnp.zeros((2, samples - taps.shape[1]), jnp.float32),
-            flipped[:, :half_taps],
-        ],
-        axis=1,
-    )
     chunk_rows = block_count * block_rows // halves
     share = taus // subsets
     rows_z = tiles // 2
-    smem = pl.BlockSpec(memory_space=pltpu.SMEM)
     vmem = pl.BlockSpec(memory_space=pltpu.VMEM)
     hbm = pl.BlockSpec(memory_space=pl.ANY)
     image = pl.pallas_call(
-        functools.partial(migrate_kernel, rows_z, subsets, half_taps),
+        functools.partial(migrate_kernel, rows_z, subsets),
         out_shape=jax.ShapeDtypeStruct((share, columns), jnp.float32),
-        in_specs=[smem, smem, vmem, hbm, hbm, hbm],
+        in_specs=[hbm] * 6,
         out_specs=vmem,
         scratch_shapes=[
             pltpu.VMEM((tiles, halves, chunk_rows, samples), jnp.bfloat16),
@@ -310,20 +358,27 @@
             pltpu.VMEM((2 * samples, chunk_rows), jnp.bfloat16),
             pltpu.VMEM((taus, columns), jnp.float32),
             pltpu.VMEM((subsets - 1, share, columns), jnp.float32),
+            pltpu.SMEM(counts.shape, jnp.int32),
+            pltpu.VMEM(aperture.shape, jnp.int32),
+            pltpu.VMEM(taps.shape, taps.dtype),
+            pltpu.VMEM((8, samples), jnp.float32),
+            pltpu.VMEM((8, slots), jnp.int32),
+            pltpu.SMEM((8, slots), jnp.int32),
             pltpu.SemaphoreType.DMA((tiles, halves)),
             pltpu.SemaphoreType.DMA((2, rows_z, halves)),
             pltpu.SemaphoreType.DMA((rows_z, halves)),
-            pltpu.SemaphoreType.DMA((3,)),
+            pltpu.SemaphoreType.DMA((halves,)),
+            pltpu.SemaphoreType.DMA((7,)),
             pltpu.SemaphoreType.DMA((subsets - 1,)),
             pltpu.SemaphoreType.DMA((subsets - 1,)),
         ],
         compiler_params=pltpu.CompilerParams(
-            collective_id=0, has_side_effects=True, vmem_limit_bytes=48 * 1024 * 1024
+            collective_id=0, has_side_effects=True, vmem_limit_bytes=62 * 1024 * 1024
         ),
     )(
-        inv,
-        alive,
-        band,
+        counts,
+        aperture,
+        taps,
         traces.reshape(halves, chunk_rows, samples),
         time_weights[0, 0],
         amplitudes[0, 0],
@@ -419,7 +474,8 @@
 def per_device(traces, taps, aperture, counts, time_weights, amplitudes):
     tiles = lax.axis_size("tile")
     every_block = traces.shape[1] * tiles
-    form = gather_per_device if every_block == aperture.shape[2] else exchange_per_device
+    gathers = every_block == aperture.shape[2] and tiles % 4 == 0
+    form = gather_per_device if gathers else exchange_per_device
     return form(traces, taps, aperture, counts, time_weights, amplitudes)
 
 

time: 40.6 us -> 40.8 us (level)
  Pallas kernels: 33.4 us -> 39.2 us
  local copies, waits for them, and re-layouts: 5.92 us -> 1.38 us
  other arithmetic: 0.94 us -> 0 us
    pallas_call x1, Pallas kernels: 33.4 us -> 39.2 us  [gather_per_device(): pl.pallas_call(functools.partial(migrate_kernel, rows_z, subsets), out_sh...]
    unnamed x7 -> x1, local copies, waits for them, and re-layouts: 3.76 us -> 1.38 us
    dynamic_slice x1 -> x0, local copies, waits for them, and re-layouts: 1.25 us -> none  [gather_per_device(): fill = lax.dynamic_index_in_dim(counts[0], myself, 0, keepdims=False)]
    rev x1 -> x0, local copies, waits for them, and re-layouts: 0.75 us -> none  [gather_per_device(): flipped = taps[:, ::-1].astype(jnp.float32)]
    lt x1 -> x0, other arithmetic: 0.65 us -> none  [gather_per_device(): match = (listing[None, :] == blocks[:, None]) & (order < fill)[None, :]]
where the time goes in v2:
time: 40.8 us; the launch traced here: 40.6 us
  Pallas kernels  39.2 us (96%)
  local copies, waits for them, and re-layouts  1.38 us (3%)
    pallas_call x1, Pallas kernels, gather_per_device(): pl.pallas_call(functools.partial(migrate_kernel, rows_z, subsets), out_sh...  39.2 us
    unnamed x1, local copies, waits for them, and re-layouts  1.38 us

profile of v2, /device:TPU:0, one launch (start us, length us, event | category | flops | bytes accessed | tf_op | source)
XLA Modules:
  0.0 40.6 jit_solution(1329292767881025872)
XLA Ops:
  0.0 39.2 %shard_map.64 = f32[32,256]{1,0:T(8,128)} custom-call(s32[1,8]{1,0:T(1,128)} %counts_hbm.1, s32[1,8,128]{2,1,0:T(8,128)} %aperture_hbm.1, bf16[2,65]{1,0:T(2,128)(2,1)} %taps_hbm.1, bf16[2,256,256]{2,1,0:T(8,128)(2,1)} %bitcast.6, bf16[128,128,256]{2,1,0:T(8,128)(2,1)} %bitcast.4, bf16[128,2,32,256]{3,2,1,0:T(8,128)(2,1)} %bitcast.5), custom_call_target="tpu_custom_call" | custom-call | tf_op jit(solution)/shard_map/pallas_call | solution.py:348
  39.2 1.4 %copy.8 = f32[1,32,256]{2,1,0:T(8,128)} copy(f32[1,32,256]{2,1,0:T(8,128)} %bitcast.7) | data formatting | bytes 65536

commit v3 on v2

--- a/solution.py
+++ b/solution.py
@@ -10,7 +10,7 @@
 group_slots = 8
 lane_group = 4
 halves = 2
-relay_from = 1
+relay_from = 2
 MESH = pl.DeviceIdType.MESH
 
 
@@ -251,33 +251,37 @@
                         def _():
                             send_x(origin_z, half).start()
 
-        if distance == 2:
-            for half in range(relay_from, halves):
-                relay(half).start()
-
-        def column_chunk(event, carry):
-            half = event // 2
-            up = event % 2
-            near = z - distance * (2 * up - 1)
-            far = z - (distance - 1) * (2 * up - 1)
-
-            @pl.when((near >= 0) & (near < rows_z))
-            def _():
-                compute(near * 2 + x, half)
-
-            if distance > 1:
+            def column_chunk(event, carry):
+                half = event // 2
+                up = event % 2
+                near = z - distance * (2 * up - 1)
+                far = z - (distance - 1) * (2 * up - 1)
+
+                @pl.when((near >= 0) & (near < rows_z))
+                def _():
+                    compute(near * 2 + x, half)
+
                 wanted = (far >= 0) & (far < rows_z)
-            else:
-                wanted = up == 1
-
-            @pl.when(wanted)
-            def _():
-                wait_arrival(far * 2 + other, half)
-                compute(far * 2 + other, half)
-
-            return carry
-
-        lax.fori_loop(0, 2 * halves, column_chunk, 0)
+                if distance == 1:
+                    wanted = up == 1
+                if distance == 2:
+                    wanted = wanted & ((half < relay_from) | (far != pair_z))
+
+                @pl.when(wanted)
+                def _():
+                    wait_arrival(far * 2 + other, half)
+                    compute(far * 2 + other, half)
+
+                return carry
+
+            lax.fori_loop(2 * half, 2 * half + 2, column_chunk, 0)
+
+    def relayed_chunk(half, carry):
+        wait_arrival(pair_z * 2 + other, half)
+        compute(pair_z * 2 + other, half)
+        return carry
+
+    lax.fori_loop(relay_from, halves, relayed_chunk, 0)
 
     share = out_ref.shape[0]
     sends = []
@@ -332,6 +336,10 @@
 
     for half in range(relay_from, halves):
         relay(half).wait_send()
+
+
+def keep(array):
+    return pltpu.with_memory_space_constraint(array, pltpu.HBM)
 
 
 def gather_per_device(traces, taps, aperture, counts, time_weights, amplitudes):
@@ -373,15 +381,15 @@
             pltpu.SemaphoreType.DMA((subsets - 1,)),
         ],
         compiler_params=pltpu.CompilerParams(
-            collective_id=0, has_side_effects=True, vmem_limit_bytes=62 * 1024 * 1024
+            collective_id=0, has_side_effects=True, vmem_limit_bytes=48 * 1024 * 1024
         ),
     )(
-        counts,
-        aperture,
-        taps,
-        traces.reshape(halves, chunk_rows, samples),
-        time_weights[0, 0],
-        amplitudes[0, 0],
+        keep(counts),
+        keep(aperture),
+        keep(taps),
+        keep(traces.reshape(halves, chunk_rows, samples)),
+        keep(time_weights[0, 0]),
+        keep(amplitudes[0, 0]),
     )
     return image[None]
 

time: 40.8 us -> 33.9 us (0.83)
  Pallas kernels: 39.2 us -> 33.1 us
  local copies, waits for them, and re-layouts: 1.38 us -> 0.62 us
    pallas_call x1, Pallas kernels: 39.2 us -> 33.1 us  [gather_per_device(): pl.pallas_call(functools.partial(migrate_kernel, rows_z, subsets), out_sh...]
    unnamed x1, local copies, waits for them, and re-layouts: 1.38 us -> 0.62 us
where the time goes in v3:
time: 33.9 us; the launch traced here: 33.8 us
  Pallas kernels  33.1 us (98%)
  local copies, waits for them, and re-layouts  0.62 us (2%)
    pallas_call x1, Pallas kernels, gather_per_device(): pl.pallas_call(functools.partial(migrate_kernel, rows_z, subsets), out_sh...  33.1 us

profile of v3, /device:TPU:0, one launch (start us, length us, event | category | flops | bytes accessed | tf_op | source)
XLA Modules:
  0.0 33.8 jit_solution(10816251563050678204)
XLA Ops:
  0.0 33.1 %shard_map.64 = f32[32,256]{1,0:T(8,128)S(1)} custom-call(s32[1,8]{1,0:T(1,128)} %counts_hbm.1, s32[1,8,128]{2,1,0:T(8,128)} %aperture_hbm.1, bf16[2,65]{1,0:T(2,128)(2,1)} %taps_hbm.1, bf16[2,256,256]{2,1,0:T(8,128)(2,1)} %bitcast.7, bf16[128,128,256]{2,1,0:T(8,128)(2,1)} %bitcast.5, bf16[128,2,32,256]{3,2,1,0:T(8,128)(2,1)} %bitcast.6), custom_call_target="tpu_custom_call" | custom-call | tf_op jit(solution)/shard_map/pallas_call | solution.py:356
  33.1 0.6 %copy.8 = f32[1,32,256]{2,1,0:T(8,128)} copy(f32[1,32,256]{2,1,0:T(8,128)S(1)} %bitcast.4) | data formatting | bytes 65536

commit v4 on v3

--- a/solution.py
+++ b/solution.py
@@ -10,7 +10,7 @@
 group_slots = 8
 lane_group = 4
 halves = 2
-relay_from = 2
+pieces = 2
 MESH = pl.DeviceIdType.MESH
 
 
@@ -40,7 +40,6 @@
     recv_sem,
     send_z_sem,
     send_x_sem,
-    relay_sem,
     load_sem,
     part_send_sem,
     part_recv_sem,
@@ -88,64 +87,58 @@
     inner = jnp.where((z > 0) & (z < rows_z - 1), 1, 0)
     pl.semaphore_wait(barrier, subsets + 1 + inner)
 
-    def source(origin_z, half, own):
+    units = halves * pieces
+    piece_rows = chunk_rows // pieces
+
+    def place(unit):
+        return unit // pieces, pl.ds((unit % pieces) * piece_rows, piece_rows)
+
+    def source(origin_z, unit, own):
         if own:
-            return traces_ref.at[half]
-        return gathered.at[origin_z * 2 + x, half]
-
-    def send_z(origin_z, half, up, own=False):
+            return traces_ref.at[place(unit)]
+        return gathered.at[(origin_z * 2 + x, *place(unit))]
+
+    def send_z(origin_z, unit, up, own=False):
         return pltpu.make_async_remote_copy(
-            src_ref=source(origin_z, half, own),
-            dst_ref=gathered.at[origin_z * 2 + x, half],
-            send_sem=send_z_sem.at[up, origin_z, half],
-            recv_sem=recv_sem.at[origin_z * 2 + x, half],
+            src_ref=source(origin_z, unit, own),
+            dst_ref=gathered.at[(origin_z * 2 + x, *place(unit))],
+            send_sem=send_z_sem.at[up, origin_z, unit],
+            recv_sem=recv_sem.at[origin_z * 2 + x, unit],
             device_id=(tile + 4 * up - 2, subset),
             device_id_type=MESH,
         )
 
-    def send_x(origin_z, half, own=False):
+    def send_x(origin_z, unit, own=False):
         return pltpu.make_async_remote_copy(
-            src_ref=source(origin_z, half, own),
-            dst_ref=gathered.at[origin_z * 2 + x, half],
-            send_sem=send_x_sem.at[origin_z, half],
-            recv_sem=recv_sem.at[origin_z * 2 + x, half],
+            src_ref=source(origin_z, unit, own),
+            dst_ref=gathered.at[(origin_z * 2 + x, *place(unit))],
+            send_sem=send_x_sem.at[origin_z, unit],
+            recv_sem=recv_sem.at[origin_z * 2 + x, unit],
             device_id=(z * 2 + other, subset),
             device_id_type=MESH,
         )
 
-    pair_z = z + 1 - 2 * (z % 2)
-
-    def relay(half):
-        return pltpu.make_async_remote_copy(
-            src_ref=gathered.at[z * 2 + other, half],
-            dst_ref=gathered.at[z * 2 + other, half],
-            send_sem=relay_sem.at[half],
-            recv_sem=recv_sem.at[z * 2 + other, half],
-            device_id=(pair_z * 2 + x, subset),
-            device_id_type=MESH,
-        )
-
-    def wait_arrival(origin, half):
+    def wait_arrival(origin, unit):
         pltpu.make_async_remote_copy(
-            src_ref=gathered.at[origin, half],
-            dst_ref=gathered.at[origin, half],
+            src_ref=gathered.at[(origin, *place(unit))],
+            dst_ref=gathered.at[(origin, *place(unit))],
             send_sem=send_x_sem.at[0, 0],
-            recv_sem=recv_sem.at[origin, half],
+            recv_sem=recv_sem.at[origin, unit],
             device_id=(z * 2 + other, subset),
             device_id_type=MESH,
         ).wait_recv()
 
-    for half in range(halves):
+    for unit in range(units):
 
         @pl.when(z < rows_z - 1)
         def _():
-            send_z(z, half, 1, True).start()
+            send_z(z, unit, 1, True).start()
 
         @pl.when(z > 0)
         def _():
-            send_z(z, half, 0, True).start()
-
-        send_x(z, half, True).start()
+            send_z(z, unit, 0, True).start()
+
+        send_x(z, unit, True).start()
 
     load_weights.start()
     load_spread.start()
@@ -232,24 +225,19 @@
 
     for distance in range(1, rows_z + 1):
         for half in range(halves):
-            for up in (1, 0):
-                origin_z = z - distance if up else z + distance
-
-                @pl.when((origin_z >= 0) & (origin_z < rows_z))
-                def _():
-                    wait_arrival(origin_z * 2 + x, half)
-
-                    @pl.when((z > 0) & (z < rows_z - 1))
+            for unit in range(half * pieces, (half + 1) * pieces):
+                for up in (1, 0):
+                    origin_z = z - distance if up else z + distance
+
+                    @pl.when((origin_z >= 0) & (origin_z < rows_z))
                     def _():
-                        send_z(origin_z, half, up).start()
-
-                    if half < relay_from:
-                        send_x(origin_z, half).start()
-                    else:
-
-                        @pl.when(origin_z != pair_z)
+                        wait_arrival(origin_z * 2 + x, unit)
+
+                        @pl.when((z > 0) & (z < rows_z - 1))
                         def _():
-                            send_x(origin_z, half).start()
+                            send_z(origin_z, unit, up).start()
+
+                        send_x(origin_z, unit).start()
 
             def column_chunk(event, carry):
                 half = event // 2
@@ -264,24 +252,16 @@
                 wanted = (far >= 0) & (far < rows_z)
                 if distance == 1:
                     wanted = up == 1
-                if distance == 2:
-                    wanted = wanted & ((half < relay_from) | (far != pair_z))
 
                 @pl.when(wanted)
                 def _():
-                    wait_arrival(far * 2 + other, half)
+                    for piece in range(pieces):
+                        wait_arrival(far * 2 + other, half * pieces + piece)
                     compute(far * 2 + other, half)
 
                 return carry
 
             lax.fori_loop(2 * half, 2 * half + 2, column_chunk, 0)
-
-    def relayed_chunk(half, carry):
-        wait_arrival(pair_z * 2 + other, half)
-        compute(pair_z * 2 + other, half)
-        return carry
-
-    lax.fori_loop(relay_from, halves, relayed_chunk, 0)
 
     share = out_ref.shape[0]
     sends = []
@@ -305,17 +285,17 @@
     for copy in sends:
         copy.wait_send()
 
-    for half in range(halves):
+    for unit in range(units):
 
         @pl.when(z < rows_z - 1)
         def _():
-            send_z(z, half, 1, True).wait_send()
+            send_z(z, unit, 1, True).wait_send()
 
         @pl.when(z > 0)
         def _():
-            send_z(z, half, 0, True).wait_send()
-
-        send_x(z, half, True).wait_send()
+            send_z(z, unit, 0, True).wait_send()
+
+        send_x(z, unit, True).wait_send()
         for distance in range(1, rows_z):
             for up in (1, 0):
                 origin_z = z - distance if up else z + distance
@@ -324,18 +304,9 @@
                 def _():
                     @pl.when((z > 0) & (z < rows_z - 1))
                     def _():
-                        send_z(origin_z, half, up).wait_send()
-
-                    if half < relay_from:
-                        send_x(origin_z, half).wait_send()
-                    else:
-
-                        @pl.when(origin_z != pair_z)
-                        def _():
-                            send_x(origin_z, half).wait_send()
-
-    for half in range(relay_from, halves):
-        relay(half).wait_send()
+                        send_z(origin_z, unit, up).wait_send()
+
+                    send_x(origin_z, unit).wait_send()
 
 
 def keep(array):
@@ -351,6 +322,7 @@
     chunk_rows = block_count * block_rows // halves
     share = taus // subsets
     rows_z = tiles // 2
+    units = halves * pieces
     vmem = pl.BlockSpec(memory_space=pltpu.VMEM)
     hbm = pl.BlockSpec(memory_space=pl.ANY)
     image = pl.pallas_call(
@@ -372,10 +344,9 @@
             pltpu.VMEM((8, samples), jnp.float32),
             pltpu.VMEM((8, slots), jnp.int32),
             pltpu.SMEM((8, slots), jnp.int32),
-            pltpu.SemaphoreType.DMA((tiles, halves)),
-            pltpu.SemaphoreType.DMA((2, rows_z, halves)),
-            pltpu.SemaphoreType.DMA((rows_z, halves)),
-            pltpu.SemaphoreType.DMA((halves,)),
+            pltpu.SemaphoreType.DMA((tiles, units)),
+            pltpu.SemaphoreType.DMA((2, rows_z, units)),
+            pltpu.SemaphoreType.DMA((rows_z, units)),
             pltpu.SemaphoreType.DMA((7,)),
             pltpu.SemaphoreType.DMA((subsets - 1,)),
             pltpu.SemaphoreType.DMA((subsets - 1,)),

time: 33.9 us -> 34.3 us (1.012)
  Pallas kernels: 33.1 us -> 33.5 us
    pallas_call x1, Pallas kernels: 33.1 us -> 33.5 us  [gather_per_device(): pl.pallas_call(functools.partial(migrate_kernel, rows_z, subsets), out_sh...]
where the time goes in v4:
time: 34.3 us; the launch traced here: 34.1 us
  Pallas kernels  33.5 us (98%)
  local copies, waits for them, and re-layouts  0.62 us (2%)
    pallas_call x1, Pallas kernels, gather_per_device(): pl.pallas_call(functools.partial(migrate_kernel, rows_z, subsets), out_sh...  33.5 us

profile of v4, /device:TPU:0, one launch (start us, length us, event | category | flops | bytes accessed | tf_op | source)
XLA Modules:
  0.0 34.1 jit_solution(11815405226672890303)
XLA Ops:
  0.0 33.5 %shard_map.64 = f32[32,256]{1,0:T(8,128)S(1)} custom-call(s32[1,8]{1,0:T(1,128)} %counts_hbm.1, s32[1,8,128]{2,1,0:T(8,128)} %aperture_hbm.1, bf16[2,65]{1,0:T(2,128)(2,1)} %taps_hbm.1, bf16[2,256,256]{2,1,0:T(8,128)(2,1)} %bitcast.7, bf16[128,128,256]{2,1,0:T(8,128)(2,1)} %bitcast.5, bf16[128,2,32,256]{3,2,1,0:T(8,128)(2,1)} %bitcast.6), custom_call_target="tpu_custom_call" | custom-call | tf_op jit(solution)/shard_map/pallas_call | solution.py:328
  33.5 0.6 %copy.8 = f32[1,32,256]{2,1,0:T(8,128)} copy(f32[1,32,256]{2,1,0:T(8,128)S(1)} %bitcast.4) | data formatting | bytes 65536
